TPU v7x, 512 devices: a whole 4x4x16 slice. The times are simulated.
512 devices in a mesh: mp: 64 (over x, z), replica: 8 (over y, core).
Axes of the slice: x: 4, y: 4, z: 16, core: 2. Of those that a mesh axis runs over, the one named last changes fastest.
Arguments:
- pooled_grads: bfloat16 [64, 8, 128, 64, 128], P('mp', 'replica'), may hold values from -0.119628906 to 0.119628906
- table: float32 [64, 512, 128], P('mp'), may hold values from -3 to 3
- state: float32 [64, 512], P('mp'), may hold values from 0.2 to 5
- tile_mult: bfloat16 [64, 8, 64, 128, 128], P('mp', 'replica'), may hold values from 0 to 3, as said below
- tile_rows: int32 [64, 8, 64], P('mp', 'replica'), may hold values from 0 to 3
Outputs:
- new_table: float32 [64, 512, 128], P('mp')
- new_state: float32 [64, 512], P('mp')
Inputs may be any that keep to these rules, and one draw needn't show every extreme that they name: tile_mult holds whole numbers.
All inputs are finite; a program needn't handle non-finite values.
Results may differ from a plain program's by a relative error of at most 0.0003.
Values may be sent and summed in bfloat16 or wider, within the bound.
No kernel may reach another device: no remote copies, remote signals or barrier semaphores. Data moves between devices by JAX's collectives and lax.ppermute only.
A program may use at most 64 MiB of HBM per device.

v0:
```python
import jax
import jax.numpy as jnp
from jax import lax
from jax.sharding import PartitionSpec as P

LEARN_RATE = 0.5
EPSILON = 1e-06


def adagrad(weights_in, accum_in, gradient):
    accum_out = accum_in + jnp.mean(gradient * gradient, axis=-1)
    weights_out = weights_in - LEARN_RATE * gradient / (jnp.sqrt(accum_out)[..., None] + EPSILON)
    return (weights_out, accum_out)


def on_device(pooled_grads, table, state, tile_mult, tile_rows):
    local_grads = pooled_grads[0, 0]
    width = local_grads.shape[-1]
    received = lax.all_to_all(local_grads, "mp", split_axis=1, concat_axis=0, tiled=True)
    counts_bf = tile_mult[0, 0]
    block_size = counts_bf.shape[-1]
    sample_blocks = received.reshape(-1, block_size, width)
    row_ids = tile_rows[0, 0]
    contrib = jnp.einsum(
        "tsr,tse->tre", counts_bf, sample_blocks, preferred_element_type=jnp.float32
    )
    weights_in = table[0]
    accum_in = state[0]
    row_count = weights_in.shape[0]
    row_blocks = row_count // block_size
    onehot = (row_ids[:, None] == jnp.arange(row_blocks, dtype=jnp.int32)[None, :]).astype(
        jnp.float32
    )
    partial_grad = jnp.einsum(
        "tb,tre->bre", onehot, contrib, precision=lax.Precision.HIGHEST
    ).reshape(row_count, width)
    total_grad = lax.psum(partial_grad, "replica")
    weights_out, accum_out = adagrad(weights_in, accum_in, total_grad)
    return (weights_out[None], accum_out[None])


def solution(mesh):
    placed = (
        P("mp", "replica", None, None, None),
        P("mp", None, None),
        P("mp", None),
        P("mp", "replica", None, None, None),
        P("mp", "replica", None),
    )
    return jax.shard_map(
        on_device,
        mesh=mesh,
        in_specs=placed,
        out_specs=(P("mp", None, None), P("mp", None)),
        check_vma=False,
    )
```

profile of v0, /device:TPU:2, one launch (start us, length us, event | category | flops | bytes accessed | tf_op | source)
XLA Modules:
  0.0 211.9 jit_solution(7404038184944069721)
XLA Ops:
  7.2 0.0 copy-start
  7.2 0.0 all-reduce.2.cloned.1.call-start
  7.2 3.1 %copy.16 = bf16[1,1,128,64,128]{4,2,3,1,0:T(8,128)(2,1)S(1)} copy(bf16[1,1,128,64,128]{4,3,2,1,0:T(8,128)(2,1)} %param.5) | data formatting | bytes 4194304 | tf_op args[0]
  10.3 115.6 %all_to_all.15 = bf16[128,64,128]{2,0,1:T(8,128)(2,1)S(1)} all-to-all(bf16[128,64,128]{2,0,1:T(8,128)(2,1)S(1)} %bitcast.26), channel_id=1, replica_groups=mesh['mp'=64,'replica'=8] {'mp'}, dimensions={1} | all-to-all | bytes 4194304 | tf_op jit(solution)/shard_map/all_to_all | solution.py:19
  125.9 0.0 copy-done
  125.9 0.0 copy-start.3
  126.0 0.9 fusion.2
  126.8 0.0 copy-done.3
  126.8 0.0 copy-start.2
  126.9 0.0 copy-start.1
  126.9 3.8 %fusion = f32[4,128,128]{2,0,1:T(4,128)S(1)} fusion(f32[64,128,128]{2,1,0:T(8,128)S(1)} %fusion.2, s32[64]{0:T(128)S(1)} %bitcast.30), kind=kOutput, calls=%fused_computation | convolution fusion | flops 50331904 | bytes 4456704 | tf_op jit(solution)/shard_map/tb,tre->bre/dot_general | solution.py:34
  130.7 0.7 copy.11
  131.4 0.0 all-reduce.2.cloned.1.call-update
  131.4 70.1 %all-reduce.2.cloned.1.call-done = f32[512,128]{1,0:T(8,128)} async-done(((f32[512,128]{1,0:T(8,128)}), f32[512,128]{1,0:T(8,128)}) %all-reduce.2.cloned.1.call-update) | async-done | bytes 262160 | tf_op jit(solution)/shard_map/psum | solution.py:37
  201.5 1.1 multiply_reduce_fusion
  202.6 0.0 copy-done.2
  202.6 0.6 add.26
  203.2 0.0 copy-done.1
  203.2 1.8 fusion.5
  (1 shorter events, 0.0 us)
Async XLA Ops:
  7.2 118.8 %copy-start = (bf16[1,1,64,128,128]{4,3,2,1,0:T(8,128)(2,1)S(1)}, bf16[1,1,64,128,128]{4,3,2,1,0:T(8,128)(2,1)}, u32[]{:S(2)}) copy-start(bf16[1,1,64,128,128]{4,3,2,1,0:T(8,128)(2,1)} %param.8) | copy-start | bytes 6291460
  7.2 194.3 %all-reduce.2.cloned.1.call-start = ((), (), s32[]{:S(2)}) async-start(), calls=%async_computation.1 | async-start | bytes 524288 | tf_op jit(solution)/shard_map/psum | solution.py:37
  125.9 0.9 copy-start.3
  126.8 75.8 %copy-start.2 = (f32[1,512]{1,0:T(1,128)S(1)}, f32[1,512]{1,0:T(1,128)}, u32[]{:S(2)}) copy-start(f32[1,512]{1,0:T(1,128)} %param.7) | copy-start | bytes 6148
  126.9 76.4 %copy-start.1 = (f32[1,512,128]{2,1,0:T(8,128)S(1)}, f32[1,512,128]{2,1,0:T(8,128)}, u32[]{:S(2)}) copy-start(f32[1,512,128]{2,1,0:T(8,128)} %param.6) | copy-start | bytes 786436
Sparse Core Ops, SparseCore 0:
  131.5 69.9 all-reduce.1
where the time goes:
time: 212 us
  blocking collectives  116 us (55%)
  waiting for transfers between devices  70.1 us (33%)
  between operations  14.1 us (7%)
  matrix products  4.67 us (2%)
  local copies, waits for them, and re-layouts  3.83 us (2%)
  other arithmetic  3.48 us (2%)
    all_to_all x1, blocking collectives, on_device(): lax.all_to_all(local_grads, 'mp', split_axis=1, concat_axis=0, tiled=True)  116 us
    psum x1, waiting for transfers between devices, on_device(): total_grad = lax.psum(partial_grad, 'replica')  70.1 us
  transfers between devices with their start and end apart: 1, of which 1 were waited for; matrix products, arithmetic and copies ran while one was open for 0% of the time, Pallas kernels for 0%

commit v1 on v0

--- a/solution.py
+++ b/solution.py
@@ -5,6 +5,15 @@
 
 LEARN_RATE = 0.5
 EPSILON = 1e-06
+
+
+def balance_the_trees(mine):
+    wide_out = mine
+    n_parts = lax.axis_size("replica")
+    for k0 in [m for m in (1, 2, 4, 8, 16) if m < n_parts]:
+        block_now = lax.ppermute(wide_out, "replica", [(p, p ^ k0) for p in range(n_parts)])
+        wide_out = wide_out + block_now
+    return wide_out
 
 
 def adagrad(weights_in, accum_in, gradient):
@@ -34,7 +43,7 @@
     partial_grad = jnp.einsum(
         "tb,tre->bre", onehot, contrib, precision=lax.Precision.HIGHEST
     ).reshape(row_count, width)
-    total_grad = lax.psum(partial_grad, "replica")
+    total_grad = balance_the_trees(partial_grad)
     weights_out, accum_out = adagrad(weights_in, accum_in, total_grad)
     return (weights_out[None], accum_out[None])
 

time: 212 us -> 151 us (0.71)
  the two profiles are of different devices: /device:TPU:2 before, /device:TPU:38 now
where the time goes in v1:
time: 151 us
  blocking collectives  116 us (77%)
  waiting for transfers between devices  14 us (9%)
  starting transfers between devices  10.6 us (7%)
  matrix products  4.67 us (3%)
  local copies, waits for them, and re-layouts  3.13 us (2%)
  other arithmetic  1.64 us (1%)
    all_to_all x1, blocking collectives, on_device(): lax.all_to_all(local_grads, 'mp', split_axis=1, concat_axis=0, tiled=True)  116 us
    ppermute x3, waiting for transfers between devices, balance_the_trees(): lax.ppermute(wide_out, 'replica', [(p, p ^ k0) for p in range(n_parts)])  14 us
    ppermute x3, starting transfers between devices, balance_the_trees(): lax.ppermute(wide_out, 'replica', [(p, p ^ k0) for p in range(n_parts)])  10.6 us
    dot_general x1, matrix products, on_device(): jnp.einsum('tb,tre->bre', onehot, contrib, precision=lax.Precision.HIGHEST)  3.8 us
    unnamed x9, local copies, waits for them, and re-layouts  3.12 us
  transfers between devices with their start and end apart: 3, of which 3 were waited for; matrix products, arithmetic and copies ran while one was open for 0% of the time, Pallas kernels for 0%

profile of v1, /device:TPU:38, one launch (start us, length us, event | category | flops | bytes accessed | tf_op | source)
XLA Modules:
  0.0 151.1 jit_solution(3645059440562759108)
XLA Ops:
  0.6 0.0 copy-start
  0.6 3.1 %copy.16 = bf16[1,1,128,64,128]{4,2,3,1,0:T(8,128)(2,1)S(1)} copy(bf16[1,1,128,64,128]{4,3,2,1,0:T(8,128)(2,1)} %param.5) | data formatting | bytes 4194304 | tf_op args[0]
  3.7 116.3 %all_to_all.15 = bf16[128,64,128]{2,0,1:T(8,128)(2,1)S(1)} all-to-all(bf16[128,64,128]{2,0,1:T(8,128)(2,1)S(1)} %bitcast.27), channel_id=1, replica_groups=mesh['mp'=64,'replica'=8] {'mp'}, dimensions={1} | all-to-all | bytes 4194304 | tf_op jit(solution)/shard_map/all_to_all | solution.py:28
  120.0 0.0 copy-done
  120.0 0.0 copy-start.3
  120.0 0.9 fusion.2
  120.9 0.0 copy-done.3
  120.9 3.8 %fusion = f32[4,128,128]{2,0,1:T(4,128)S(1)} fusion(f32[64,128,128]{2,1,0:T(8,128)S(1)} %fusion.2, s32[64]{0:T(128)S(1)} %bitcast.31), kind=kOutput, calls=%fused_computation | convolution fusion | flops 50331904 | bytes 4456704 | tf_op jit(solution)/shard_map/tb,tre->bre/dot_general | solution.py:43
  124.7 0.0 copy-start.2
  124.7 0.0 copy-start.1
  124.8 2.1 %collective-permute-start = (f32[512,128]{1,0:T(8,128)S(1)}, f32[512,128]{1,0:T(8,128)S(1)}, u32[]{:S(2)}, u32[]{:S(2)}) collective-permute-start(f32[512,128]{1,0:T(8,128)S(1)} %bitcast.28), channel_id=1, source_target_pairs={{0,1},{1,0},{2,3},{3,2},{4,5},{5,4},{6,7},{7,6},{8,9},{9,8},{10,11... | collective-permute-start | bytes 786440 | tf_op jit(solution)/shard_map/ppermute | solution.py:14
  126.8 1.5 collective-permute-done
  128.3 3.5 %collective-permute-start.1 = (f32[512,128]{1,0:T(8,128)S(1)}, f32[512,128]{1,0:T(8,128)S(1)}, u32[]{:S(2)}, u32[]{:S(2)}) collective-permute-start(f32[512,128]{1,0:T(8,128)S(1)} %bitcast_add_fusion), channel_id=1, source_target_pairs={{0,2},{1,3},{2,0},{3,1},{4,6},{5,7},{6,4},{7,5},{8,10},{9,11},{10,... | collective-permute-start | bytes 786440 | tf_op jit(solution)/shard_map/ppermute | solution.py:14
  131.8 6.7 %collective-permute-done.1 = f32[512,128]{1,0:T(8,128)S(1)} collective-permute-done((f32[512,128]{1,0:T(8,128)S(1)}, f32[512,128]{1,0:T(8,128)S(1)}, u32[]{:S(2)}, u32[]{:S(2)}) %collective-permute-start.1) | collective-permute-done | bytes 262176 | tf_op jit(solution)/shard_map/ppermute | solution.py:14
  138.6 5.1 %collective-permute-start.2 = (f32[512,128]{1,0:T(8,128)S(1)}, f32[512,128]{1,0:T(8,128)S(1)}, u32[]{:S(2)}, u32[]{:S(2)}) collective-permute-start(f32[512,128]{1,0:T(8,128)S(1)} %add.31), channel_id=1, source_target_pairs={{0,4},{1,5},{2,6},{3,7},{4,0},{5,1},{6,2},{7,3},{8,12},{9,13},{10,... | collective-permute-start | bytes 786440 | tf_op jit(solution)/shard_map/ppermute | solution.py:14
  143.7 5.8 %collective-permute-done.2 = f32[512,128]{1,0:T(8,128)S(1)} collective-permute-done((f32[512,128]{1,0:T(8,128)S(1)}, f32[512,128]{1,0:T(8,128)S(1)}, u32[]{:S(2)}, u32[]{:S(2)}) %collective-permute-start.2) | collective-permute-done | bytes 262176 | tf_op jit(solution)/shard_map/ppermute | solution.py:14
  149.5 0.1 multiply_reduce_fusion
  149.7 0.0 copy-done.2
  149.7 0.6 add.36
  150.3 0.0 copy-done.1
  150.3 0.8 fusion.5
  (4 shorter events, 0.1 us)
Async XLA Ops:
  0.6 119.4 %copy-start = (bf16[1,1,64,128,128]{4,3,2,1,0:T(8,128)(2,1)S(1)}, bf16[1,1,64,128,128]{4,3,2,1,0:T(8,128)(2,1)}, u32[]{:S(2)}) copy-start(bf16[1,1,64,128,128]{4,3,2,1,0:T(8,128)(2,1)} %param.8) | copy-start | bytes 6291460
  120.0 0.9 copy-start.3
  124.7 25.0 %copy-start.2 = (f32[1,512]{1,0:T(1,128)S(1)}, f32[1,512]{1,0:T(1,128)}, u32[]{:S(2)}) copy-start(f32[1,512]{1,0:T(1,128)} %param.7) | copy-start | bytes 6148
  124.7 25.6 %copy-start.1 = (f32[1,512,128]{2,1,0:T(8,128)S(1)}, f32[1,512,128]{2,1,0:T(8,128)}, u32[]{:S(2)}) copy-start(f32[1,512,128]{2,1,0:T(8,128)} %param.6) | copy-start | bytes 786436
  124.8 3.6 %collective-permute-start = (f32[512,128]{1,0:T(8,128)S(1)}, f32[512,128]{1,0:T(8,128)S(1)}, u32[]{:S(2)}, u32[]{:S(2)}) collective-permute-start(f32[512,128]{1,0:T(8,128)S(1)} %bitcast.28), channel_id=1, source_target_pairs={{0,1},{1,0},{2,3},{3,2},{4,5},{5,4},{6,7},{7,6},{8,9},{9,8},{10,11... | collective-permute-start | bytes 786440 | tf_op jit(solution)/shard_map/ppermute | solution.py:14
  128.3 10.2 %collective-permute-start.1 = (f32[512,128]{1,0:T(8,128)S(1)}, f32[512,128]{1,0:T(8,128)S(1)}, u32[]{:S(2)}, u32[]{:S(2)}) collective-permute-start(f32[512,128]{1,0:T(8,128)S(1)} %bitcast_add_fusion), channel_id=1, source_target_pairs={{0,2},{1,3},{2,0},{3,1},{4,6},{5,7},{6,4},{7,5},{8,10},{9,11},{10,... | collective-permute-start | bytes 786440 | tf_op jit(solution)/shard_map/ppermute | solution.py:14
  138.6 10.9 %collective-permute-start.2 = (f32[512,128]{1,0:T(8,128)S(1)}, f32[512,128]{1,0:T(8,128)S(1)}, u32[]{:S(2)}, u32[]{:S(2)}) collective-permute-start(f32[512,128]{1,0:T(8,128)S(1)} %add.31), channel_id=1, source_target_pairs={{0,4},{1,5},{2,6},{3,7},{4,0},{5,1},{6,2},{7,3},{8,12},{9,13},{10,... | collective-permute-start | bytes 786440 | tf_op jit(solution)/shard_map/ppermute | solution.py:14
